TPU v7x, 32 devices: a whole 2x2x4 slice. The times are simulated.
32 devices in a mesh: gx: 4 (over z), gy: 8 (over y, x, core).
Axes of the slice: x: 2, y: 2, z: 4, core: 2. Of those that a mesh axis runs over, the one named last changes fastest.
Arguments:
- orbitals: bfloat16 [24, 48, 11, 256], P('gx', 'gy'), may hold values from -140 to 140, as said below
- masses: float32 [24, 48, 11], P('gx', 'gy'), may hold values from 0.5 to 2, as said below
- cell_matrices: bfloat16 [4, 8, 2, 216, 216], P('gx', 'gy'), may hold values from -0.12 to 3.12, as said below
Outputs:
- filtered_orbitals: bfloat16 [24, 48, 11, 256], P('gx', 'gy')
Inputs may be any that keep to these rules, and one draw needn't show every extreme that they name: Entries of orbitals that hold the same mesh node are equal. Entries of masses that hold the same mesh node are equal. `cell_matrices`: every cell matrix is symmetric.
All inputs are finite; a program needn't handle non-finite values.
Results may differ from a plain program's by a relative error of at most 0.0063.
The roundings to bfloat16 on the way count: a program that leaves them out, or rounds other values in their place, can miss the bound.
Values sent between devices are 32-bit elements; how exact they have to be, the bound alone decides.
A program may use at most 64 MiB of HBM per device.

v0:
```python
import jax
import jax.numpy as jnp
from jax import lax
from jax.sharding import PartitionSpec as P

FILTER_DEG = 3
NS_STEPS = 2
center_shift = 12.0
half_span = 12.0


def with_halo(array, sides, width):
    for axis, dim in sides:
        size, length = (lax.axis_size(axis), array.shape[dim])
        up = [(i, (i + 1) % size) for i in range(size)]
        down = [(j, i) for i, j in up]
        last = lax.slice_in_dim(array, length - width, length, axis=dim)
        leading = lax.slice_in_dim(array, 0, width, axis=dim)
        before = lax.ppermute(last, axis, up)
        after = lax.ppermute(leading, axis, down)
        array = jnp.concatenate([before, array, after], axis=dim)
    return array


def unfold_cells(values, along_dim, cells_along):
    moved = jnp.moveaxis(values, along_dim, 0)
    trailing = moved.shape[1:]
    main_part = moved[: 5 * cells_along].reshape((cells_along, 5) + trailing)
    far_layer = moved[5::5][:, None]
    window = jnp.concatenate([main_part, far_layer], 1)
    return jnp.moveaxis(window, (0, 1), (along_dim, along_dim + 1))


def fold_cells(window, along_dim, cells_along):
    moved = jnp.moveaxis(window, (along_dim, along_dim + 1), (0, 1))
    trailing = moved.shape[2:]
    leading = jnp.concatenate([moved[:, :5], jnp.zeros((1, 5) + trailing, moved.dtype)], 0)
    carried = jnp.concatenate([jnp.zeros((1,) + trailing, moved.dtype), moved[:, 5]], 0)
    leading = leading.at[:, 0].add(carried)
    flattened = leading.reshape((5 * (cells_along + 1),) + trailing)[: 5 * cells_along + 1]
    return jnp.moveaxis(flattened, 0, along_dim)


def to_cells(values, cells_x, cells_y, cells_z):
    window = unfold_cells(values, 0, cells_x)
    window = unfold_cells(window, 2, cells_y)
    window = unfold_cells(window, 4, cells_z)
    window = jnp.transpose(window, (0, 2, 4, 1, 3, 5, 6))
    return window.reshape((cells_x, cells_y, cells_z, 216, window.shape[-1]))


def from_cells(products, cells_x, cells_y, cells_z):
    window = products.reshape((cells_x, cells_y, cells_z, 6, 6, 6, products.shape[-1]))
    window = jnp.transpose(window, (0, 3, 1, 4, 2, 5, 6))
    window = fold_cells(window, 4, cells_z)
    window = fold_cells(window, 2, cells_y)
    return fold_cells(window, 0, cells_x)


def inverse_root(intersection):
    frob_norm = jnp.sqrt(jnp.sum(intersection * intersection))
    current = intersection / frob_norm
    identity = jnp.eye(intersection.shape[0], dtype=jnp.float32)
    factor_z = identity
    for sweep_index in range(NS_STEPS):
        step_t = 1.5 * identity - 0.5 * jnp.dot(factor_z, current, precision=lax.Precision.HIGHEST)
        current = jnp.dot(current, step_t, precision=lax.Precision.HIGHEST)
        factor_z = jnp.dot(step_t, factor_z, precision=lax.Precision.HIGHEST)
    return factor_z / jnp.sqrt(frob_norm)


def body(orbitals, masses, cell_matrices):
    cells_x, cells_y, cells_z = cell_matrices.shape[:3]
    orb_count = orbitals.shape[3]

    def apply_operator(rounded):
        cell_vectors = to_cells(rounded, cells_x, cells_y, cells_z)
        products = jnp.einsum(
            "abcij,abcjo->abcio", cell_matrices, cell_vectors, preferred_element_type=jnp.float32
        )
        partial_value = from_cells(products, cells_x, cells_y, cells_z)
        padded = with_halo(partial_value, (("gx", 0), ("gy", 1)), 1)
        summed = partial_value.at[0].add(padded[0, 1:-1]).at[-1].add(padded[-1, 1:-1])
        summed = summed.at[:, 0].add(padded[1:-1, 0]).at[:, -1].add(padded[1:-1, -1])
        summed = summed.at[0, 0].add(padded[0, 0]).at[0, -1].add(padded[0, -1])
        summed = summed.at[-1, 0].add(padded[-1, 0]).at[-1, -1].add(padded[-1, -1])
        return summed / masses[..., None]

    starting = orbitals.astype(jnp.float32)
    previous = starting
    current = (apply_operator(orbitals) - center_shift * starting) / half_span
    for sweep_index in range(FILTER_DEG - 1):
        following = (
            2.0
            * (apply_operator(current.astype(jnp.bfloat16)) - center_shift * current)
            / half_span
            - previous
        )
        previous = current
        current = following
    owned_rows = current[:-1, :-1].reshape((-1, orb_count))
    owned_mass = masses[:-1, :-1].reshape((-1, 1))
    local_intersection = jnp.einsum(
        "no,np->op", owned_rows * owned_mass, owned_rows, precision=lax.Precision.HIGHEST
    )
    node_total = (
        (current.shape[0] - 1)
        * lax.axis_size("gx")
        * (current.shape[1] - 1)
        * lax.axis_size("gy")
        * current.shape[2]
    )
    row_sum = lax.psum(local_intersection, "gy")
    intersection_sum = lax.psum(row_sum, "gx")
    intersection = intersection_sum / node_total
    factor = inverse_root(intersection)
    node_rows = current.reshape((-1, orb_count))
    result = jnp.dot(node_rows, factor, precision=lax.Precision.HIGHEST).astype(jnp.bfloat16)
    return result.reshape(current.shape)


def solution(mesh):
    return jax.shard_map(
        body,
        mesh=mesh,
        in_specs=(P("gx", "gy", None, None), P("gx", "gy", None), P("gx", "gy", None, None, None)),
        out_specs=P("gx", "gy", None, None),
        check_vma=False,
    )
```

profile of v0, /device:TPU:0, one launch (start us, length us, event | category | flops | bytes accessed | tf_op | source)
XLA Modules:
  0.0 195.6 jit_solution(4431525838171367299)
XLA Ops:
  6.5 1.0 copy-done.1
  8.3 0.3 pad_maximum_fusion
  9.6 0.6 copy.62
  10.1 0.3 slice_bitcast_fusion.5
  10.4 0.2 slice.1356
  10.7 0.5 copy-done.2
  11.4 0.6 slice-done.1
  12.4 0.7 copy.65
  13.1 0.3 slice_bitcast_fusion.4
  13.9 0.2 concatenate.167
  14.5 3.1 %collective-permute-start = (f32[1,6,11,256]{3,2,1,0:T(8,128)S(1)}, f32[1,6,11,256]{3,2,1,0:T(8,128)S(1)}, u32[]{:S(2)}, u32[]{:S(2)}) collective-permute-start(f32[1,6,11,256]{3,2,1,0:T(8,128)S(1)} %slice.1363), channel_id=1, source_target_pairs={{0,8},{8,16},{16,24},{24,0},{1,9},{9,17},{17,25},{25,1},{2,10},{10... | collective-permute-start | bytes 202760 | tf_op jit(solution)/shard_map/ppermute | solution.py:19
  17.7 0.6 copy-done.7
  18.3 0.7 and_reduce_fusion
  19.0 3.4 %collective-permute-done = f32[1,6,11,256]{3,2,1,0:T(8,128)S(1)} collective-permute-done((f32[1,6,11,256]{3,2,1,0:T(8,128)S(1)}, f32[1,6,11,256]{3,2,1,0:T(8,128)S(1)}, u32[]{:S(2)}, u32[]{:S(2)}) %collective-permute-start) | collective-permute-done | bytes 67616 | tf_op jit(solution)/shard_map/ppermute | solution.py:19
  22.4 1.9 collective-permute-start.1
  24.3 0.6 fusion.50
  24.8 2.2 %collective-permute-done.1 = f32[1,6,11,256]{3,2,1,0:T(8,128)S(1)} collective-permute-done((f32[1,6,11,256]{3,2,1,0:T(8,128)S(1)}, f32[1,6,11,256]{3,2,1,0:T(8,128)S(1)}, u32[]{:S(2)}, u32[]{:S(2)}) %collective-permute-start.1) | collective-permute-done | bytes 67616 | tf_op jit(solution)/shard_map/ppermute | solution.py:20
  27.1 2.6 %collective-permute-start.3 = (f32[8,1,11,256]{3,2,1,0:T(8,128)S(1)}, f32[8,1,11,256]{3,2,1,0:T(8,128)S(1)}, u32[]{:S(2)}, u32[]{:S(2)}) collective-permute-start(f32[8,1,11,256]{3,2,1,0:T(8,128)S(1)} %get-tuple-element.411), channel_id=1, source_target_pairs={{1,0},{2,1},{3,2},{4,3},{5,4},{6,5},{7,6},{0,7},{9,8},{10,9},{11,1... | collective-permute-start | bytes 270344 | tf_op jit(solution)/shard_map/ppermute | solution.py:20
  29.8 2.6 %collective-permute-done.2 = f32[8,1,11,256]{3,2,1,0:T(8,128)S(1)} collective-permute-done((f32[8,1,11,256]{3,2,1,0:T(8,128)S(1)}, f32[8,1,11,256]{3,2,1,0:T(8,128)S(1)}, u32[]{:S(2)}, u32[]{:S(2)}) %collective-permute-start.2) | collective-permute-done | bytes 90144 | tf_op jit(solution)/shard_map/ppermute | solution.py:19
  32.5 1.9 fusion.32
  34.5 0.7 copy-done.5
  35.5 0.3 slice.1285
  37.2 0.6 copy.76
  37.8 0.3 slice_bitcast_fusion.3
  38.3 0.5 copy-done.3
  39.1 0.6 slice-done.2
  40.0 0.7 copy.79
  40.7 0.3 slice_bitcast_fusion.2
  41.0 0.2 slice.1387
  41.5 0.2 concatenate.178
  42.3 7.1 %collective-permute-done.4 = f32[1,6,11,256]{3,2,1,0:T(8,128)S(1)} collective-permute-done((f32[1,6,11,256]{3,2,1,0:T(8,128)S(1)}, f32[1,6,11,256]{3,2,1,0:T(8,128)S(1)}, u32[]{:S(2)}, u32[]{:S(2)}) %collective-permute-start.4) | collective-permute-done | bytes 67616 | tf_op jit(solution)/shard_map/ppermute | solution.py:19
  49.4 1.9 collective-permute-start.5
  51.3 3.0 %collective-permute-done.5 = f32[1,6,11,256]{3,2,1,0:T(8,128)S(1)} collective-permute-done((f32[1,6,11,256]{3,2,1,0:T(8,128)S(1)}, f32[1,6,11,256]{3,2,1,0:T(8,128)S(1)}, u32[]{:S(2)}, u32[]{:S(2)}) %collective-permute-start.5) | collective-permute-done | bytes 67616 | tf_op jit(solution)/shard_map/ppermute | solution.py:20
  54.4 2.6 %collective-permute-start.7 = (f32[8,1,11,256]{3,2,1,0:T(8,128)S(1)}, f32[8,1,11,256]{3,2,1,0:T(8,128)S(1)}, u32[]{:S(2)}, u32[]{:S(2)}) collective-permute-start(f32[8,1,11,256]{3,2,1,0:T(8,128)S(1)} %get-tuple-element.409), channel_id=1, source_target_pairs={{1,0},{2,1},{3,2},{4,3},{5,4},{6,5},{7,6},{0,7},{9,8},{10,9},{11,1... | collective-permute-start | bytes 270344 | tf_op jit(solution)/shard_map/ppermute | solution.py:20
  57.0 3.1 %collective-permute-done.6 = f32[8,1,11,256]{3,2,1,0:T(8,128)S(1)} collective-permute-done((f32[8,1,11,256]{3,2,1,0:T(8,128)S(1)}, f32[8,1,11,256]{3,2,1,0:T(8,128)S(1)}, u32[]{:S(2)}, u32[]{:S(2)}) %collective-permute-start.6) | collective-permute-done | bytes 90144 | tf_op jit(solution)/shard_map/ppermute | solution.py:19
  60.2 1.9 fusion.33
  62.2 0.3 fusion.46
  62.6 0.3 slice.1319
  64.3 0.6 copy.89
  64.9 0.3 slice_bitcast_fusion.1
  65.2 0.2 slice.1412
  65.4 0.5 copy-done.4
  66.2 0.6 slice-done.3
  67.1 0.7 copy.92
  67.8 0.3 slice_bitcast_fusion
  68.6 0.2 concatenate.188
  69.4 7.0 %collective-permute-done.8 = f32[1,6,11,256]{3,2,1,0:T(8,128)S(1)} collective-permute-done((f32[1,6,11,256]{3,2,1,0:T(8,128)S(1)}, f32[1,6,11,256]{3,2,1,0:T(8,128)S(1)}, u32[]{:S(2)}, u32[]{:S(2)}) %collective-permute-start.8) | collective-permute-done | bytes 67616 | tf_op jit(solution)/shard_map/ppermute | solution.py:19
  76.3 2.0 %collective-permute-start.9 = (f32[1,6,11,256]{3,2,1,0:T(8,128)S(1)}, f32[1,6,11,256]{3,2,1,0:T(8,128)S(1)}, u32[]{:S(2)}, u32[]{:S(2)}) collective-permute-start(f32[1,6,11,256]{3,2,1,0:T(8,128)S(1)} %get-tuple-element.401), channel_id=1, source_target_pairs={{8,0},{16,8},{24,16},{0,24},{9,1},{17,9},{25,17},{1,25},{10,2},{18... | collective-permute-start | bytes 202760 | tf_op jit(solution)/shard_map/ppermute | solution.py:20
  78.4 2.9 %collective-permute-done.9 = f32[1,6,11,256]{3,2,1,0:T(8,128)S(1)} collective-permute-done((f32[1,6,11,256]{3,2,1,0:T(8,128)S(1)}, f32[1,6,11,256]{3,2,1,0:T(8,128)S(1)}, u32[]{:S(2)}, u32[]{:S(2)}) %collective-permute-start.9) | collective-permute-done | bytes 67616 | tf_op jit(solution)/shard_map/ppermute | solution.py:20
  81.3 2.6 %collective-permute-start.11 = (f32[8,1,11,256]{3,2,1,0:T(8,128)S(1)}, f32[8,1,11,256]{3,2,1,0:T(8,128)S(1)}, u32[]{:S(2)}, u32[]{:S(2)}) collective-permute-start(f32[8,1,11,256]{3,2,1,0:T(8,128)S(1)} %get-tuple-element.407), channel_id=1, source_target_pairs={{1,0},{2,1},{3,2},{4,3},{5,4},{6,5},{7,6},{0,7},{9,8},{10,9},{11,1... | collective-permute-start | bytes 270344 | tf_op jit(solution)/shard_map/ppermute | solution.py:20
  84.0 3.9 %collective-permute-done.10 = f32[8,1,11,256]{3,2,1,0:T(8,128)S(1)} collective-permute-done((f32[8,1,11,256]{3,2,1,0:T(8,128)S(1)}, f32[8,1,11,256]{3,2,1,0:T(8,128)S(1)}, u32[]{:S(2)}, u32[]{:S(2)}) %collective-permute-start.10) | collective-permute-done | bytes 90144 | tf_op jit(solution)/shard_map/ppermute | solution.py:19
  87.9 1.9 fusion.34
  89.9 0.4 multiply_subtract_fusion
  90.3 1.9 convolution_bitcast_fusion.3
  92.2 53.8 %all-reduce.21.cloned.1.call-done = f32[256,256]{1,0:T(8,128)} async-done(((f32[256,256]{1,0:T(8,128)}), f32[256,256]{1,0:T(8,128)}) %all-reduce.21.cloned.1.call-update) | async-done | bytes 262160 | tf_op jit(solution)/shard_map/psum | solution.py:113
  146.1 37.1 %all-reduce.23.cloned.1.call-done = f32[256,256]{1,0:T(8,128)} async-done(((f32[256,256]{1,0:T(8,128)}), f32[256,256]{1,0:T(8,128)}) %all-reduce.23.cloned.1.call-update) | async-done | bytes 262160 | tf_op jit(solution)/shard_map/psum | solution.py:114
  183.2 1.7 multiply_reduce_fusion
  185.6 0.3 fusion.1
  185.9 0.3 fusion.5
  186.2 0.4 fusion.31
  186.6 0.4 fusion
  187.0 0.4 convolution_divide_fusion
  187.4 0.5 convolution_convert_fusion
  188.0 0.8 copy.95
  (144 shorter events, 9.8 us)
Async XLA Ops:
  6.5 2.0 %copy-start = (bf16[1,1,2,216,216]{4,3,2,1,0:T(8,128)(2,1)S(1)}, bf16[1,1,2,216,216]{4,3,2,1,0:T(8,128)(2,1)}, u32[]{:S(2)}) copy-start(bf16[1,1,2,216,216]{4,3,2,1,0:T(8,128)(2,1)} %param.71) | copy-start | bytes 559876
  6.5 1.0 copy-start.1
  6.5 1.1 slice-start
  6.5 139.5 %all-reduce.21.cloned.1.call-start = ((), (), s32[]{:S(2)}) async-start(), calls=%async_computation | async-start | bytes 524288 | tf_op jit(solution)/shard_map/psum | solution.py:113
  10.4 0.8 copy-start.2
  11.2 0.9 slice-start.1
  14.5 7.9 %collective-permute-start = (f32[1,6,11,256]{3,2,1,0:T(8,128)S(1)}, f32[1,6,11,256]{3,2,1,0:T(8,128)S(1)}, u32[]{:S(2)}, u32[]{:S(2)}) collective-permute-start(f32[1,6,11,256]{3,2,1,0:T(8,128)S(1)} %slice.1363), channel_id=1, source_target_pairs={{0,8},{8,16},{16,24},{24,0},{1,9},{9,17},{17,25},{25,1},{2,10},{10... | collective-permute-start | bytes 202760 | tf_op jit(solution)/shard_map/ppermute | solution.py:19
  17.6 0.7 copy-start.7
  22.4 4.7 %collective-permute-start.1 = (f32[1,6,11,256]{3,2,1,0:T(8,128)S(1)}, f32[1,6,11,256]{3,2,1,0:T(8,128)S(1)}, u32[]{:S(2)}, u32[]{:S(2)}) collective-permute-start(f32[1,6,11,256]{3,2,1,0:T(8,128)S(1)} %get-tuple-element.405), channel_id=1, source_target_pairs={{8,0},{16,8},{24,16},{0,24},{9,1},{17,9},{25,17},{1,25},{10,2},{18... | collective-permute-start | bytes 202760 | tf_op jit(solution)/shard_map/ppermute | solution.py:20
  27.1 5.3 %collective-permute-start.2 = (f32[8,1,11,256]{3,2,1,0:T(8,128)S(1)}, f32[8,1,11,256]{3,2,1,0:T(8,128)S(1)}, u32[]{:S(2)}, u32[]{:S(2)}) collective-permute-start(f32[8,1,11,256]{3,2,1,0:T(8,128)S(1)} %get-tuple-element.412), channel_id=1, source_target_pairs={{0,1},{1,2},{2,3},{3,4},{4,5},{5,6},{6,7},{7,0},{8,9},{9,10},{10,1... | collective-permute-start | bytes 270344 | tf_op jit(solution)/shard_map/ppermute | solution.py:19
  27.1 5.3 %collective-permute-start.3 = (f32[8,1,11,256]{3,2,1,0:T(8,128)S(1)}, f32[8,1,11,256]{3,2,1,0:T(8,128)S(1)}, u32[]{:S(2)}, u32[]{:S(2)}) collective-permute-start(f32[8,1,11,256]{3,2,1,0:T(8,128)S(1)} %get-tuple-element.411), channel_id=1, source_target_pairs={{1,0},{2,1},{3,2},{4,3},{5,4},{6,5},{7,6},{0,7},{9,8},{10,9},{11,1... | collective-permute-start | bytes 270344 | tf_op jit(solution)/shard_map/ppermute | solution.py:20
  34.5 0.7 copy-start.5
  38.1 0.8 copy-start.3
  38.9 0.9 slice-start.2
  42.1 7.3 %collective-permute-start.4 = (f32[1,6,11,256]{3,2,1,0:T(8,128)S(1)}, f32[1,6,11,256]{3,2,1,0:T(8,128)S(1)}, u32[]{:S(2)}, u32[]{:S(2)}) collective-permute-start(f32[1,6,11,256]{3,2,1,0:T(8,128)S(1)} %slice.1391), channel_id=1, source_target_pairs={{0,8},{8,16},{16,24},{24,0},{1,9},{9,17},{17,25},{25,1},{2,10},{10... | collective-permute-start | bytes 202760 | tf_op jit(solution)/shard_map/ppermute | solution.py:19
  49.4 4.9 %collective-permute-start.5 = (f32[1,6,11,256]{3,2,1,0:T(8,128)S(1)}, f32[1,6,11,256]{3,2,1,0:T(8,128)S(1)}, u32[]{:S(2)}, u32[]{:S(2)}) collective-permute-start(f32[1,6,11,256]{3,2,1,0:T(8,128)S(1)} %get-tuple-element.403), channel_id=1, source_target_pairs={{8,0},{16,8},{24,16},{0,24},{9,1},{17,9},{25,17},{1,25},{10,2},{18... | collective-permute-start | bytes 202760 | tf_op jit(solution)/shard_map/ppermute | solution.py:20
  54.3 5.8 %collective-permute-start.6 = (f32[8,1,11,256]{3,2,1,0:T(8,128)S(1)}, f32[8,1,11,256]{3,2,1,0:T(8,128)S(1)}, u32[]{:S(2)}, u32[]{:S(2)}) collective-permute-start(f32[8,1,11,256]{3,2,1,0:T(8,128)S(1)} %get-tuple-element.410), channel_id=1, source_target_pairs={{0,1},{1,2},{2,3},{3,4},{4,5},{5,6},{6,7},{7,0},{8,9},{9,10},{10,1... | collective-permute-start | bytes 270344 | tf_op jit(solution)/shard_map/ppermute | solution.py:19
  54.4 5.8 %collective-permute-start.7 = (f32[8,1,11,256]{3,2,1,0:T(8,128)S(1)}, f32[8,1,11,256]{3,2,1,0:T(8,128)S(1)}, u32[]{:S(2)}, u32[]{:S(2)}) collective-permute-start(f32[8,1,11,256]{3,2,1,0:T(8,128)S(1)} %get-tuple-element.409), channel_id=1, source_target_pairs={{1,0},{2,1},{3,2},{4,3},{5,4},{6,5},{7,6},{0,7},{9,8},{10,9},{11,1... | collective-permute-start | bytes 270344 | tf_op jit(solution)/shard_map/ppermute | solution.py:20
  65.2 0.8 copy-start.4
  65.9 0.9 slice-start.3
  69.2 7.1 %collective-permute-start.8 = (f32[1,6,11,256]{3,2,1,0:T(8,128)S(1)}, f32[1,6,11,256]{3,2,1,0:T(8,128)S(1)}, u32[]{:S(2)}, u32[]{:S(2)}) collective-permute-start(f32[1,6,11,256]{3,2,1,0:T(8,128)S(1)} %slice.1419), channel_id=1, source_target_pairs={{0,8},{8,16},{16,24},{24,0},{1,9},{9,17},{17,25},{25,1},{2,10},{10... | collective-permute-start | bytes 202760 | tf_op jit(solution)/shard_map/ppermute | solution.py:19
  76.3 4.9 %collective-permute-start.9 = (f32[1,6,11,256]{3,2,1,0:T(8,128)S(1)}, f32[1,6,11,256]{3,2,1,0:T(8,128)S(1)}, u32[]{:S(2)}, u32[]{:S(2)}) collective-permute-start(f32[1,6,11,256]{3,2,1,0:T(8,128)S(1)} %get-tuple-element.401), channel_id=1, source_target_pairs={{8,0},{16,8},{24,16},{0,24},{9,1},{17,9},{25,17},{1,25},{10,2},{18... | collective-permute-start | bytes 202760 | tf_op jit(solution)/shard_map/ppermute | solution.py:20
  81.3 6.6 %collective-permute-start.10 = (f32[8,1,11,256]{3,2,1,0:T(8,128)S(1)}, f32[8,1,11,256]{3,2,1,0:T(8,128)S(1)}, u32[]{:S(2)}, u32[]{:S(2)}) collective-permute-start(f32[8,1,11,256]{3,2,1,0:T(8,128)S(1)} %get-tuple-element.408), channel_id=1, source_target_pairs={{0,1},{1,2},{2,3},{3,4},{4,5},{5,6},{6,7},{7,0},{8,9},{9,10},{10,1... | collective-permute-start | bytes 270344 | tf_op jit(solution)/shard_map/ppermute | solution.py:19
  81.3 6.6 %collective-permute-start.11 = (f32[8,1,11,256]{3,2,1,0:T(8,128)S(1)}, f32[8,1,11,256]{3,2,1,0:T(8,128)S(1)}, u32[]{:S(2)}, u32[]{:S(2)}) collective-permute-start(f32[8,1,11,256]{3,2,1,0:T(8,128)S(1)} %get-tuple-element.407), channel_id=1, source_target_pairs={{1,0},{2,1},{3,2},{4,3},{5,4},{6,5},{7,6},{0,7},{9,8},{10,9},{11,1... | collective-permute-start | bytes 270344 | tf_op jit(solution)/shard_map/ppermute | solution.py:20
  92.2 91.0 %all-reduce.23.cloned.1.call-start = ((), (), s32[]{:S(2)}) async-start(), calls=%async_computation.1 | async-start | bytes 524288 | tf_op jit(solution)/shard_map/psum | solution.py:114
  183.2 2.4 %copy-start.6 = (f32[256,256]{1,0:T(8,128)S(1)}, f32[256,256]{1,0:T(8,128)}, u32[]{:S(2)}) copy-start(f32[256,256]{1,0:T(8,128)} %all-reduce.23.cloned.1.call-done) | copy-start | bytes 786436
Sparse Core Ops, SparseCore 0:
  92.3 53.6 all-reduce.20
  148.4 34.6 all-reduce.22
where the time goes:
time: 196 us
  waiting for transfers between devices  126 us (64%)
  local copies, waits for them, and re-layouts  21 us (11%)
  starting transfers between devices  17.1 us (9%)
  between operations  15.3 us (8%)
  other arithmetic  11.6 us (6%)
  matrix products  4.74 us (2%)
    psum x1, waiting for transfers between devices, body(): row_sum = lax.psum(local_intersection, 'gy')  53.8 us
    psum x1, waiting for transfers between devices, body(): intersection_sum = lax.psum(row_sum, 'gx')  37.1 us
    ppermute x6, waiting for transfers between devices, with_halo(): before = lax.ppermute(last, axis, up)  27 us
    ppermute x6, starting transfers between devices, with_halo(): after = lax.ppermute(leading, axis, down)  13.6 us
    ppermute x6, waiting for transfers between devices, with_halo(): after = lax.ppermute(leading, axis, down)  8.1 us
    scatter-add x6, other arithmetic, apply_operator(): summed = summed.at[0, 0].add(padded[0, 0]).at[0, -1].add(padded[0, -1])  5.81 us
    unnamed x26, local copies, waits for them, and re-layouts  5.14 us
    scatter-add x9, local copies, waits for them, and re-layouts, fold_cells(): leading = leading.at[:, 0].add(carried)  4.14 us
  transfers between devices with their start and end apart: 14, of which 11 were waited for; matrix products, arithmetic and copies ran while one was open for 1% of the time, Pallas kernels for 0%

commit v1 on v0

--- a/solution.py
+++ b/solution.py
@@ -111,7 +111,8 @@
         * current.shape[2]
     )
     row_sum = lax.psum(local_intersection, "gy")
-    intersection_sum = lax.psum(row_sum, "gx")
+    parts = lax.all_gather(row_sum, "gx", axis=0, tiled=False)
+    intersection_sum = parts.sum(axis=0)
     intersection = intersection_sum / node_total
     factor = inverse_root(intersection)
     node_rows = current.reshape((-1, orb_count))

time: 196 us -> 188 us (0.959)
  waiting for transfers between devices: 126 us -> 118 us
    psum x1 -> x0, waiting for transfers between devices: 37.1 us -> none  [body(): intersection_sum = lax.psum(row_sum, 'gx')]
    all_gather x0 -> x1, waiting for transfers between devices: none -> 28.9 us  [body(): parts = lax.all_gather(row_sum, 'gx', axis=0, tiled=False)]
    unnamed x26 -> x24, local copies, waits for them, and re-layouts: 5.14 us -> 5.13 us
where the time goes in v1:
time: 188 us
  waiting for transfers between devices  118 us (63%)
  local copies, waits for them, and re-layouts  20.9 us (11%)
  starting transfers between devices  17.1 us (9%)
  between operations  15.3 us (8%)
  other arithmetic  11.8 us (6%)
  matrix products  4.73 us (3%)
    psum x1, waiting for transfers between devices, body(): row_sum = lax.psum(local_intersection, 'gy')  53.8 us
    all_gather x1, waiting for transfers between devices, body(): parts = lax.all_gather(row_sum, 'gx', axis=0, tiled=False)  28.9 us
    ppermute x6, waiting for transfers between devices, with_halo(): before = lax.ppermute(last, axis, up)  27 us
    ppermute x6, starting transfers between devices, with_halo(): after = lax.ppermute(leading, axis, down)  13.6 us
    ppermute x6, waiting for transfers between devices, with_halo(): after = lax.ppermute(leading, axis, down)  8.1 us
    scatter-add x6, other arithmetic, apply_operator(): summed = summed.at[0, 0].add(padded[0, 0]).at[0, -1].add(padded[0, -1])  5.67 us
    unnamed x24, local copies, waits for them, and re-layouts  5.13 us
    scatter-add x9, local copies, waits for them, and re-layouts, fold_cells(): leading = leading.at[:, 0].add(carried)  4.14 us
  transfers between devices with their start and end apart: 14, of which 11 were waited for; matrix products, arithmetic and copies ran while one was open for 1% of the time, Pallas kernels for 0%

profile of v1, /device:TPU:0, one launch (start us, length us, event | category | flops | bytes accessed | tf_op | source)
XLA Modules:
  0.0 187.6 jit_solution(2126964210829399947)
XLA Ops:
  6.5 1.0 copy-done.1
  8.3 0.3 pad_maximum_fusion
  9.6 0.6 copy.146
  10.1 0.3 slice_bitcast_fusion.5
  10.7 0.5 copy-done.2
  11.2 0.2 concatenate.165
  11.4 0.6 slice-done.1
  12.4 0.7 copy.149
  13.1 0.3 slice_bitcast_fusion.4
  13.4 0.2 slice.1359
  13.9 0.2 concatenate.167
  14.5 3.1 %collective-permute-start = (f32[1,6,11,256]{3,2,1,0:T(8,128)S(1)}, f32[1,6,11,256]{3,2,1,0:T(8,128)S(1)}, u32[]{:S(2)}, u32[]{:S(2)}) collective-permute-start(f32[1,6,11,256]{3,2,1,0:T(8,128)S(1)} %slice.1363), channel_id=1, source_target_pairs={{0,8},{8,16},{16,24},{24,0},{1,9},{9,17},{17,25},{25,1},{2,10},{10... | collective-permute-start | bytes 202760 | tf_op jit(solution)/shard_map/ppermute | solution.py:19
  17.7 0.6 copy-done.6
  18.3 0.8 and_reduce_fusion
  19.0 3.3 %collective-permute-done = f32[1,6,11,256]{3,2,1,0:T(8,128)S(1)} collective-permute-done((f32[1,6,11,256]{3,2,1,0:T(8,128)S(1)}, f32[1,6,11,256]{3,2,1,0:T(8,128)S(1)}, u32[]{:S(2)}, u32[]{:S(2)}) %collective-permute-start) | collective-permute-done | bytes 67616 | tf_op jit(solution)/shard_map/ppermute | solution.py:19
  22.4 1.9 collective-permute-start.1
  24.3 0.6 fusion.50
  24.8 2.2 %collective-permute-done.1 = f32[1,6,11,256]{3,2,1,0:T(8,128)S(1)} collective-permute-done((f32[1,6,11,256]{3,2,1,0:T(8,128)S(1)}, f32[1,6,11,256]{3,2,1,0:T(8,128)S(1)}, u32[]{:S(2)}, u32[]{:S(2)}) %collective-permute-start.1) | collective-permute-done | bytes 67616 | tf_op jit(solution)/shard_map/ppermute | solution.py:20
  27.1 2.6 %collective-permute-start.3 = (f32[8,1,11,256]{3,2,1,0:T(8,128)S(1)}, f32[8,1,11,256]{3,2,1,0:T(8,128)S(1)}, u32[]{:S(2)}, u32[]{:S(2)}) collective-permute-start(f32[8,1,11,256]{3,2,1,0:T(8,128)S(1)} %get-tuple-element.411), channel_id=1, source_target_pairs={{1,0},{2,1},{3,2},{4,3},{5,4},{6,5},{7,6},{0,7},{9,8},{10,9},{11,1... | collective-permute-start | bytes 270344 | tf_op jit(solution)/shard_map/ppermute | solution.py:20
  29.8 2.6 %collective-permute-done.2 = f32[8,1,11,256]{3,2,1,0:T(8,128)S(1)} collective-permute-done((f32[8,1,11,256]{3,2,1,0:T(8,128)S(1)}, f32[8,1,11,256]{3,2,1,0:T(8,128)S(1)}, u32[]{:S(2)}, u32[]{:S(2)}) %collective-permute-start.2) | collective-permute-done | bytes 90144 | tf_op jit(solution)/shard_map/ppermute | solution.py:19
  32.5 1.9 %fusion.32 = f32[6,6,11,256]{3,2,1,0:T(8,128)S(1)} fusion(f32[6,6,11,256]{3,2,1,0:T(8,128)S(1)} %fusion.43, s32[]{:T(128)} %bitcast.27, s32[]{:T(128)} %bitcast.28, f32[8,1,11,256]{3,2,1,0:T(8,128)S(1)} %collective-permute-done.3, pred[]{:T(512)} %and_reduce_fusion), kind=kLoop, calls=%fused_computation.117 | loop fusion | flops 5632 | bytes 49161 | tf_op jit(solution)/shard_map/scatter-add | solution.py:85
  34.4 0.7 copy-done.5
  35.5 0.3 slice.1285
  37.2 0.6 copy.160
  37.7 0.3 slice_bitcast_fusion.3
  38.3 0.5 copy-done.3
  39.0 0.6 slice-done.2
  40.0 0.7 copy.163
  40.7 0.3 slice_bitcast_fusion.2
  41.5 0.2 concatenate.178
  42.2 7.1 %collective-permute-done.4 = f32[1,6,11,256]{3,2,1,0:T(8,128)S(1)} collective-permute-done((f32[1,6,11,256]{3,2,1,0:T(8,128)S(1)}, f32[1,6,11,256]{3,2,1,0:T(8,128)S(1)}, u32[]{:S(2)}, u32[]{:S(2)}) %collective-permute-start.4) | collective-permute-done | bytes 67616 | tf_op jit(solution)/shard_map/ppermute | solution.py:19
  49.3 1.9 collective-permute-start.5
  51.2 3.0 %collective-permute-done.5 = f32[1,6,11,256]{3,2,1,0:T(8,128)S(1)} collective-permute-done((f32[1,6,11,256]{3,2,1,0:T(8,128)S(1)}, f32[1,6,11,256]{3,2,1,0:T(8,128)S(1)}, u32[]{:S(2)}, u32[]{:S(2)}) %collective-permute-start.5) | collective-permute-done | bytes 67616 | tf_op jit(solution)/shard_map/ppermute | solution.py:20
  54.3 2.6 %collective-permute-start.7 = (f32[8,1,11,256]{3,2,1,0:T(8,128)S(1)}, f32[8,1,11,256]{3,2,1,0:T(8,128)S(1)}, u32[]{:S(2)}, u32[]{:S(2)}) collective-permute-start(f32[8,1,11,256]{3,2,1,0:T(8,128)S(1)} %get-tuple-element.409), channel_id=1, source_target_pairs={{1,0},{2,1},{3,2},{4,3},{5,4},{6,5},{7,6},{0,7},{9,8},{10,9},{11,1... | collective-permute-start | bytes 270344 | tf_op jit(solution)/shard_map/ppermute | solution.py:20
  57.0 3.1 %collective-permute-done.6 = f32[8,1,11,256]{3,2,1,0:T(8,128)S(1)} collective-permute-done((f32[8,1,11,256]{3,2,1,0:T(8,128)S(1)}, f32[8,1,11,256]{3,2,1,0:T(8,128)S(1)}, u32[]{:S(2)}, u32[]{:S(2)}) %collective-permute-start.6) | collective-permute-done | bytes 90144 | tf_op jit(solution)/shard_map/ppermute | solution.py:19
  60.2 1.9 %fusion.33 = f32[6,6,11,256]{3,2,1,0:T(8,128)S(1)} fusion(f32[6,6,11,256]{3,2,1,0:T(8,128)S(1)} %fusion.40, s32[]{:T(128)} %bitcast.27, s32[]{:T(128)} %bitcast.28, f32[8,1,11,256]{3,2,1,0:T(8,128)S(1)} %collective-permute-done.7, pred[]{:T(512)} %and_reduce_fusion), kind=kLoop, calls=%fused_computation.118 | loop fusion | flops 5632 | bytes 49161 | tf_op jit(solution)/shard_map/scatter-add | solution.py:85
  62.1 0.3 fusion.46
  62.5 0.3 slice.1319
  64.2 0.6 copy.173
  64.8 0.3 slice_bitcast_fusion.1
  65.3 0.5 copy-done.4
  66.1 0.6 slice-done.3
  67.0 0.7 copy.176
  67.7 0.3 slice_bitcast_fusion
  68.5 0.2 concatenate.188
  69.2 7.0 %collective-permute-done.8 = f32[1,6,11,256]{3,2,1,0:T(8,128)S(1)} collective-permute-done((f32[1,6,11,256]{3,2,1,0:T(8,128)S(1)}, f32[1,6,11,256]{3,2,1,0:T(8,128)S(1)}, u32[]{:S(2)}, u32[]{:S(2)}) %collective-permute-start.8) | collective-permute-done | bytes 67616 | tf_op jit(solution)/shard_map/ppermute | solution.py:19
  76.2 2.0 %collective-permute-start.9 = (f32[1,6,11,256]{3,2,1,0:T(8,128)S(1)}, f32[1,6,11,256]{3,2,1,0:T(8,128)S(1)}, u32[]{:S(2)}, u32[]{:S(2)}) collective-permute-start(f32[1,6,11,256]{3,2,1,0:T(8,128)S(1)} %get-tuple-element.401), channel_id=1, source_target_pairs={{8,0},{16,8},{24,16},{0,24},{9,1},{17,9},{25,17},{1,25},{10,2},{18... | collective-permute-start | bytes 202760 | tf_op jit(solution)/shard_map/ppermute | solution.py:20
  78.3 2.9 %collective-permute-done.9 = f32[1,6,11,256]{3,2,1,0:T(8,128)S(1)} collective-permute-done((f32[1,6,11,256]{3,2,1,0:T(8,128)S(1)}, f32[1,6,11,256]{3,2,1,0:T(8,128)S(1)}, u32[]{:S(2)}, u32[]{:S(2)}) %collective-permute-start.9) | collective-permute-done | bytes 67616 | tf_op jit(solution)/shard_map/ppermute | solution.py:20
  81.2 2.6 %collective-permute-start.11 = (f32[8,1,11,256]{3,2,1,0:T(8,128)S(1)}, f32[8,1,11,256]{3,2,1,0:T(8,128)S(1)}, u32[]{:S(2)}, u32[]{:S(2)}) collective-permute-start(f32[8,1,11,256]{3,2,1,0:T(8,128)S(1)} %get-tuple-element.407), channel_id=1, source_target_pairs={{1,0},{2,1},{3,2},{4,3},{5,4},{6,5},{7,6},{0,7},{9,8},{10,9},{11,1... | collective-permute-start | bytes 270344 | tf_op jit(solution)/shard_map/ppermute | solution.py:20
  83.9 3.9 %collective-permute-done.10 = f32[8,1,11,256]{3,2,1,0:T(8,128)S(1)} collective-permute-done((f32[8,1,11,256]{3,2,1,0:T(8,128)S(1)}, f32[8,1,11,256]{3,2,1,0:T(8,128)S(1)}, u32[]{:S(2)}, u32[]{:S(2)}) %collective-permute-start.10) | collective-permute-done | bytes 90144 | tf_op jit(solution)/shard_map/ppermute | solution.py:19
  87.8 1.9 %fusion.34 = f32[6,6,11,256]{3,2,1,0:T(8,128)S(1)} fusion(f32[6,6,11,256]{3,2,1,0:T(8,128)S(1)} %fusion.37, s32[]{:T(128)} %bitcast.27, s32[]{:T(128)} %bitcast.28, f32[8,1,11,256]{3,2,1,0:T(8,128)S(1)} %collective-permute-done.11, pred[]{:T(512)} %and_reduce_fusion), kind=kLoop, calls=%fused_computation.119 | loop fusion | flops 5632 | bytes 49161 | tf_op jit(solution)/shard_map/scatter-add | solution.py:85
  89.8 0.4 multiply_subtract_fusion
  90.1 1.9 convolution_bitcast_fusion.3
  92.1 53.8 %all-reduce.20.cloned.1.call-done = f32[1,256,256]{2,1,0:T(8,128)} async-done(((f32[1,256,256]{2,1,0:T(8,128)}), f32[1,256,256]{2,1,0:T(8,128)}) %all-reduce.20.cloned.1.call-update) | async-done | bytes 262160 | tf_op jit(solution)/shard_map/psum | solution.py:113
  146.0 28.9 %all-gather.2.cloned.1.call-done = f32[4,256,256]{2,1,0:T(8,128)} async-done(((f32[1,256,256]{2,1,0:T(8,128)}), f32[4,256,256]{2,1,0:T(8,128)}) %all-gather.2.cloned.1.call-update) | async-done | bytes 1048592 | tf_op jit(solution)/shard_map/all_gather | solution.py:114
  174.8 1.3 reduce_sum.18
  176.2 0.7 multiply_reduce_fusion
  177.5 0.3 fusion.1
  177.9 0.4 fusion.31
  178.3 0.3 fusion.5
  178.6 0.4 fusion
  179.0 0.4 convolution_divide_fusion
  179.4 0.5 convolution_convert_fusion
  180.0 0.8 copy.179
  (143 shorter events, 10.1 us)
Async XLA Ops:
  6.5 2.0 %copy-start = (bf16[1,1,2,216,216]{4,3,2,1,0:T(8,128)(2,1)S(1)}, bf16[1,1,2,216,216]{4,3,2,1,0:T(8,128)(2,1)}, u32[]{:S(2)}) copy-start(bf16[1,1,2,216,216]{4,3,2,1,0:T(8,128)(2,1)} %param.71) | copy-start | bytes 559876
  6.5 1.0 copy-start.1
  6.5 1.1 slice-start
  6.5 139.3 %all-reduce.20.cloned.1.call-start = ((), (), s32[]{:S(2)}) async-start(), calls=%async_computation | async-start | bytes 524288 | tf_op jit(solution)/shard_map/psum | solution.py:113
  10.4 0.8 copy-start.2
  11.2 0.9 slice-start.1
  14.5 7.9 %collective-permute-start = (f32[1,6,11,256]{3,2,1,0:T(8,128)S(1)}, f32[1,6,11,256]{3,2,1,0:T(8,128)S(1)}, u32[]{:S(2)}, u32[]{:S(2)}) collective-permute-start(f32[1,6,11,256]{3,2,1,0:T(8,128)S(1)} %slice.1363), channel_id=1, source_target_pairs={{0,8},{8,16},{16,24},{24,0},{1,9},{9,17},{17,25},{25,1},{2,10},{10... | collective-permute-start | bytes 202760 | tf_op jit(solution)/shard_map/ppermute | solution.py:19
  17.6 0.7 copy-start.6
  22.4 4.7 %collective-permute-start.1 = (f32[1,6,11,256]{3,2,1,0:T(8,128)S(1)}, f32[1,6,11,256]{3,2,1,0:T(8,128)S(1)}, u32[]{:S(2)}, u32[]{:S(2)}) collective-permute-start(f32[1,6,11,256]{3,2,1,0:T(8,128)S(1)} %get-tuple-element.405), channel_id=1, source_target_pairs={{8,0},{16,8},{24,16},{0,24},{9,1},{17,9},{25,17},{1,25},{10,2},{18... | collective-permute-start | bytes 202760 | tf_op jit(solution)/shard_map/ppermute | solution.py:20
  27.1 5.3 %collective-permute-start.2 = (f32[8,1,11,256]{3,2,1,0:T(8,128)S(1)}, f32[8,1,11,256]{3,2,1,0:T(8,128)S(1)}, u32[]{:S(2)}, u32[]{:S(2)}) collective-permute-start(f32[8,1,11,256]{3,2,1,0:T(8,128)S(1)} %get-tuple-element.412), channel_id=1, source_target_pairs={{0,1},{1,2},{2,3},{3,4},{4,5},{5,6},{6,7},{7,0},{8,9},{9,10},{10,1... | collective-permute-start | bytes 270344 | tf_op jit(solution)/shard_map/ppermute | solution.py:19
  27.1 5.3 %collective-permute-start.3 = (f32[8,1,11,256]{3,2,1,0:T(8,128)S(1)}, f32[8,1,11,256]{3,2,1,0:T(8,128)S(1)}, u32[]{:S(2)}, u32[]{:S(2)}) collective-permute-start(f32[8,1,11,256]{3,2,1,0:T(8,128)S(1)} %get-tuple-element.411), channel_id=1, source_target_pairs={{1,0},{2,1},{3,2},{4,3},{5,4},{6,5},{7,6},{0,7},{9,8},{10,9},{11,1... | collective-permute-start | bytes 270344 | tf_op jit(solution)/shard_map/ppermute | solution.py:20
  34.4 0.7 copy-start.5
  38.0 0.8 copy-start.3
  38.8 0.9 slice-start.2
  42.1 7.3 %collective-permute-start.4 = (f32[1,6,11,256]{3,2,1,0:T(8,128)S(1)}, f32[1,6,11,256]{3,2,1,0:T(8,128)S(1)}, u32[]{:S(2)}, u32[]{:S(2)}) collective-permute-start(f32[1,6,11,256]{3,2,1,0:T(8,128)S(1)} %slice.1391), channel_id=1, source_target_pairs={{0,8},{8,16},{16,24},{24,0},{1,9},{9,17},{17,25},{25,1},{2,10},{10... | collective-permute-start | bytes 202760 | tf_op jit(solution)/shard_map/ppermute | solution.py:19
  49.3 4.9 %collective-permute-start.5 = (f32[1,6,11,256]{3,2,1,0:T(8,128)S(1)}, f32[1,6,11,256]{3,2,1,0:T(8,128)S(1)}, u32[]{:S(2)}, u32[]{:S(2)}) collective-permute-start(f32[1,6,11,256]{3,2,1,0:T(8,128)S(1)} %get-tuple-element.403), channel_id=1, source_target_pairs={{8,0},{16,8},{24,16},{0,24},{9,1},{17,9},{25,17},{1,25},{10,2},{18... | collective-permute-start | bytes 202760 | tf_op jit(solution)/shard_map/ppermute | solution.py:20
  54.2 5.8 %collective-permute-start.6 = (f32[8,1,11,256]{3,2,1,0:T(8,128)S(1)}, f32[8,1,11,256]{3,2,1,0:T(8,128)S(1)}, u32[]{:S(2)}, u32[]{:S(2)}) collective-permute-start(f32[8,1,11,256]{3,2,1,0:T(8,128)S(1)} %get-tuple-element.410), channel_id=1, source_target_pairs={{0,1},{1,2},{2,3},{3,4},{4,5},{5,6},{6,7},{7,0},{8,9},{9,10},{10,1... | collective-permute-start | bytes 270344 | tf_op jit(solution)/shard_map/ppermute | solution.py:19
  54.3 5.8 %collective-permute-start.7 = (f32[8,1,11,256]{3,2,1,0:T(8,128)S(1)}, f32[8,1,11,256]{3,2,1,0:T(8,128)S(1)}, u32[]{:S(2)}, u32[]{:S(2)}) collective-permute-start(f32[8,1,11,256]{3,2,1,0:T(8,128)S(1)} %get-tuple-element.409), channel_id=1, source_target_pairs={{1,0},{2,1},{3,2},{4,3},{5,4},{6,5},{7,6},{0,7},{9,8},{10,9},{11,1... | collective-permute-start | bytes 270344 | tf_op jit(solution)/shard_map/ppermute | solution.py:20
  65.1 0.8 copy-start.4
  65.8 0.9 slice-start.3
  69.1 7.1 %collective-permute-start.8 = (f32[1,6,11,256]{3,2,1,0:T(8,128)S(1)}, f32[1,6,11,256]{3,2,1,0:T(8,128)S(1)}, u32[]{:S(2)}, u32[]{:S(2)}) collective-permute-start(f32[1,6,11,256]{3,2,1,0:T(8,128)S(1)} %slice.1419), channel_id=1, source_target_pairs={{0,8},{8,16},{16,24},{24,0},{1,9},{9,17},{17,25},{25,1},{2,10},{10... | collective-permute-start | bytes 202760 | tf_op jit(solution)/shard_map/ppermute | solution.py:19
  76.2 4.9 %collective-permute-start.9 = (f32[1,6,11,256]{3,2,1,0:T(8,128)S(1)}, f32[1,6,11,256]{3,2,1,0:T(8,128)S(1)}, u32[]{:S(2)}, u32[]{:S(2)}) collective-permute-start(f32[1,6,11,256]{3,2,1,0:T(8,128)S(1)} %get-tuple-element.401), channel_id=1, source_target_pairs={{8,0},{16,8},{24,16},{0,24},{9,1},{17,9},{25,17},{1,25},{10,2},{18... | collective-permute-start | bytes 202760 | tf_op jit(solution)/shard_map/ppermute | solution.py:20
  81.2 6.6 %collective-permute-start.10 = (f32[8,1,11,256]{3,2,1,0:T(8,128)S(1)}, f32[8,1,11,256]{3,2,1,0:T(8,128)S(1)}, u32[]{:S(2)}, u32[]{:S(2)}) collective-permute-start(f32[8,1,11,256]{3,2,1,0:T(8,128)S(1)} %get-tuple-element.408), channel_id=1, source_target_pairs={{0,1},{1,2},{2,3},{3,4},{4,5},{5,6},{6,7},{7,0},{8,9},{9,10},{10,1... | collective-permute-start | bytes 270344 | tf_op jit(solution)/shard_map/ppermute | solution.py:19
  81.2 6.6 %collective-permute-start.11 = (f32[8,1,11,256]{3,2,1,0:T(8,128)S(1)}, f32[8,1,11,256]{3,2,1,0:T(8,128)S(1)}, u32[]{:S(2)}, u32[]{:S(2)}) collective-permute-start(f32[8,1,11,256]{3,2,1,0:T(8,128)S(1)} %get-tuple-element.407), channel_id=1, source_target_pairs={{1,0},{2,1},{3,2},{4,3},{5,4},{6,5},{7,6},{0,7},{9,8},{10,9},{11,1... | collective-permute-start | bytes 270344 | tf_op jit(solution)/shard_map/ppermute | solution.py:20
  92.0 82.8 %all-gather.2.cloned.1.call-start = ((), (), s32[]{:S(2)}) async-start(), calls=%async_computation.1 | async-start | bytes 1310720 | tf_op jit(solution)/shard_map/all_gather | solution.py:114
Sparse Core Ops, SparseCore 0:
  92.1 53.6 all-reduce.19
  147.5 27.2 all-gather.1
